TPU v7x, 512 devices: a whole 4x4x16 slice. The times are simulated.
512 devices in a mesh: node: 128 (over z, x, core), hub: 4 (over y).
Axes of the slice: x: 4, y: 4, z: 16, core: 2. Of those that a mesh axis runs over, the one named last changes fastest.
Arguments:
- node_state: bfloat16 [32768, 256], P('node'), may hold values from -7 to 7
- w_source: bfloat16 [256, 256], replicated, may hold values from -0.375 to 0.375
- w_target: bfloat16 [256, 256], replicated, may hold values from -0.375 to 0.375
- type_table: bfloat16 [4, 256], replicated, may hold values from -5 to 5
- attention: float32 [8, 32], replicated, may hold values from -28 to 28
- w_input: bfloat16 [256, 768], replicated, may hold values from -0.375 to 0.375
- w_hidden: bfloat16 [256, 768], replicated, may hold values from -0.375 to 0.375
- edge_src: int32 [524288], P(('node', 'hub')), may hold values from 0 to 32767, as said below
- edge_dst: int32 [524288], P(('node', 'hub')), may hold values from 0 to 255, as said below
- edge_type: int32 [524288], P(('node', 'hub')), may hold values from 0 to 2, as said below
- edge_live: int32 [524288], P(('node', 'hub')), may hold values from 0 to 1, as said below
Outputs:
- new_state: bfloat16 [32768, 256], P('node')
Inputs may be any that keep to these rules, and one draw needn't show every extreme that they name: `edge_src`: A device's 1024 slots form 128 blocks of 8; the sources of block k lie in node partition k (nodes k * 256 to (k + 1) * 256 - 1). The sources of one block, live or not, are at most 2 distinct nodes, and exactly 2 in every block. `edge_dst`: destination's index within the node partition of the device. `edge_type`: the last type is never on an edge slot. `edge_live`: within each block of 8 slots the live ones come first; each block has at least one live slot, and each device has a block with all 8 live.
All inputs are finite; a program needn't handle non-finite values.
Results may differ from a plain program's by a relative error of at most 0.012.
Values may be sent and summed in bfloat16 or wider, within the bound.
A program may use at most 64 MiB of HBM per device.

v0:
```python
import jax
import jax.numpy as jnp
from jax import lax
from jax.sharding import PartitionSpec as P

big_value = 1e30


def merged_2(shard, axis, combine):
    everything = jax.tree.map(lambda part: lax.all_gather(part, axis), shard)
    first = jax.tree.map(lambda part: part[0], everything)

    def hop(k, so_far):
        return combine(so_far, jax.tree.map(lambda part: part[k], everything))

    return lax.fori_loop(1, lax.axis_size(axis), hop, first)


def attend(pre, attention):
    leaky = jnp.maximum(pre, 0.2 * pre)
    shaped = leaky.reshape(pre.shape[0], attention.shape[0], attention.shape[1])
    return jnp.sum(shaped * attention[None, :, :], axis=2)


def spread(per_head, head_dim):
    return jnp.repeat(per_head, head_dim, axis=1)


def combine(first, second):
    head_dim = first[2].shape[1] // first[0].shape[1]
    peak = jnp.maximum(first[0], second[0])
    scale_first = jnp.exp(first[0] - peak)
    scale_second = jnp.exp(second[0] - peak)
    total = first[1] * scale_first + second[1] * scale_second
    value = first[2] * spread(scale_first, head_dim) + second[2] * spread(scale_second, head_dim)
    return (peak, total, value)


def edge_partial(rows, dst, kinds, live, target, type_table, attention, node_dev):
    head_dim = attention.shape[1]
    highest = lax.Precision.HIGHEST
    member = dst[:, None] == jnp.arange(node_dev, dtype=jnp.int32)[None, :]
    onehot = member.astype(jnp.float32)
    kind_hot = (kinds[:, None] == jnp.arange(type_table.shape[0], dtype=jnp.int32)[None, :]).astype(
        jnp.bfloat16
    )
    kind_rows = jnp.dot(kind_hot, type_table, preferred_element_type=jnp.float32)
    wide_rows = rows.astype(jnp.float32)
    tgt_rows = jnp.dot(onehot, target, precision=highest, preferred_element_type=jnp.float32)
    pre = wide_rows + tgt_rows + kind_rows
    alive = live[:, None] > 0
    score = jnp.where(alive, attend(pre, attention), -big_value)
    peak = jnp.max(jnp.where(member.T[:, :, None], score[None, :, :], -big_value), axis=1)
    edge_peak = jnp.dot(onehot, peak, precision=highest, preferred_element_type=jnp.float32)
    weight = jnp.where(alive, jnp.exp(score - edge_peak), 0.0)
    total = jnp.dot(onehot.T, weight, precision=highest, preferred_element_type=jnp.float32)
    value = jnp.dot(
        onehot.T,
        spread(weight, head_dim) * wide_rows,
        precision=highest,
        preferred_element_type=jnp.float32,
    )
    return (peak, total, value)


def self_part(own, tgt, type_table, attention):
    own_rows = own.astype(jnp.float32)
    score = attend(own_rows + tgt + type_table[-1].astype(jnp.float32)[None, :], attention)
    return (score, jnp.ones_like(score), own_rows)


def recurrent(agg, state, w_input, w_hidden):
    width = state.shape[1]
    from_input = jnp.dot(agg, w_input, preferred_element_type=jnp.float32)
    from_state = jnp.dot(state, w_hidden, preferred_element_type=jnp.float32)
    reset = jax.nn.sigmoid(from_input[:, :width] + from_state[:, :width])
    update = jax.nn.sigmoid(from_input[:, width : 2 * width] + from_state[:, width : 2 * width])
    candidate = jnp.tanh(from_input[:, 2 * width :] + reset * from_state[:, 2 * width :])
    return ((1.0 - update) * candidate + update * state.astype(jnp.float32)).astype(jnp.bfloat16)


def finish_rows(merged, own, tgt, type_table, attention, state, w_input, w_hidden):
    head_dim = attention.shape[1]
    final = combine(merged, self_part(own, tgt, type_table, attention))
    agg = (final[2] / spread(final[1], head_dim)).astype(jnp.bfloat16)
    return recurrent(agg, state, w_input, w_hidden)


def body(
    node_state,
    w_source,
    w_target,
    type_table,
    attention,
    w_input,
    w_hidden,
    edge_src,
    edge_dst,
    edge_type,
    edge_live,
):
    peers = lax.axis_size("node")
    node_dev, width = node_state.shape
    heads = attention.shape[0]
    source = jnp.dot(node_state, w_source, preferred_element_type=jnp.float32).astype(jnp.bfloat16)
    target = jnp.dot(node_state, w_target, preferred_element_type=jnp.float32)
    edge_dev = edge_src.shape[0]
    slots = edge_dev // peers
    local_src = (
        edge_src.reshape(peers, slots) - (jnp.arange(peers, dtype=jnp.int32) * node_dev)[:, None]
    )
    fetched = lax.all_to_all(
        source[lax.all_to_all(local_src, "node", split_axis=0, concat_axis=0, tiled=True)],
        "node",
        split_axis=0,
        concat_axis=0,
        tiled=True,
    )
    rows = fetched.reshape(edge_dev, width)
    block = min(edge_dev, 512)
    count = edge_dev // block

    def step(carry, items):
        part_rows, part_dst, part_kinds, part_live = items
        fresh = edge_partial(
            part_rows, part_dst, part_kinds, part_live, target, type_table, attention, node_dev
        )
        return (combine(carry, fresh), None)

    start = (
        jnp.full((node_dev, heads), -big_value, jnp.float32),
        jnp.zeros((node_dev, heads), jnp.float32),
        jnp.zeros((node_dev, width), jnp.float32),
    )
    local, _ = lax.scan(
        step,
        start,
        (
            rows.reshape(count, block, width),
            edge_dst.reshape(count, block),
            edge_type.reshape(count, block),
            edge_live.reshape(count, block),
        ),
    )
    merged = merged_2(local, "hub", combine)
    return finish_rows(merged, source, target, type_table, attention, node_state, w_input, w_hidden)


def solution(mesh):
    placed = (
        P("node", None),
        P(),
        P(),
        P(),
        P(),
        P(),
        P(),
        P(("node", "hub")),
        P(("node", "hub")),
        P(("node", "hub")),
        P(("node", "hub")),
    )
    return jax.shard_map(
        body, mesh=mesh, in_specs=placed, out_specs=P("node", None), check_vma=False
    )
```

profile of v0, /device:TPU:1, one launch (start us, length us, event | category | flops | bytes accessed | tf_op | source)
XLA Modules:
  0.0 130.7 jit_solution(8336744961525355268)
XLA Ops:
  6.5 0.8 reshape.173
  7.4 0.7 broadcast_subtract_fusion
  8.1 20.4 %all-to-all-start = ((s32[128,1,8]{2,1,0:T(1,128)}), s32[128,1,8]{2,1,0:T(1,128)S(1)}, u32[]{:S(2)}, u32[]{:S(2)}) async-start(s32[128,1,8]{2,1,0:T(1,128)} %bitcast.5), calls=%async_computation | async-start | bytes 131072 | tf_op jit(solution)/shard_map/all_to_all | solution.py:113
  28.5 1.2 convolution_convert_fusion
  29.8 13.5 %all-to-all-done = s32[128,1,8]{2,1,0:T(1,128)S(1)} async-done(((s32[128,1,8]{2,1,0:T(1,128)}), s32[128,1,8]{2,1,0:T(1,128)S(1)}, u32[]{:S(2)}, u32[]{:S(2)}) %all-to-all-start) | async-done | bytes 4128 | tf_op jit(solution)/shard_map/all_to_all | solution.py:113
  43.4 5.0 %gather_fusion = bf16[1024,256]{1,0:T(8,128)(2,1)} fusion(bf16[256,256]{1,0:T(8,128)(2,1)S(1)} %copy.42, s32[1024]{0:T(1024)S(1)} %broadcast_clamp_fusion), kind=kCustom, calls=%fused_computation | custom fusion | bytes 1052672 | tf_op jit(solution)/shard_map/gather | solution.py:113
  48.4 5.9 %all-to-all-start.1 = ((bf16[128,8,256]{2,1,0:T(8,128)(2,1)}), bf16[128,8,256]{2,1,0:T(8,128)(2,1)S(1)}, u32[]{:S(2)}, u32[]{:S(2)}) async-start(bf16[128,8,256]{2,1,0:T(8,128)(2,1)} %bitcast.7), calls=%async_computation.1 | async-start | bytes 1048576 | tf_op jit(solution)/shard_map/all_to_all | solution.py:112
  54.5 0.3 multiply_reduce_fusion.1
  54.8 0.1 copy.44
  54.9 30.6 %all-to-all-done.1 = bf16[128,8,256]{2,1,0:T(8,128)(2,1)S(1)} async-done(((bf16[128,8,256]{2,1,0:T(8,128)(2,1)}), bf16[128,8,256]{2,1,0:T(8,128)(2,1)S(1)}, u32[]{:S(2)}, u32[]{:S(2)}) %all-to-all-start.1) | async-done | bytes 524320 | tf_op jit(solution)/shard_map/all_to_all | solution.py:112
  85.5 7.6 %while.35 = (s32[]{:T(128)}, f32[256,8]{0,1:T(8,128)S(1)}, f32[256,8]{0,1:T(8,128)S(1)}, f32[256,256]{1,0:T(8,128)S(1)}, s32[2,512]{1,0:T(2,128)S(1)}, /*index=5...) while((s32[]{:T(128)}, f32[256,8]{0,1:T(8,128)S(1)}, ...), condition=%wide.region_3.4_spmd.clone, body=%wide.region_0.3_spmd.clone.sunk | while | flops 835875328 | bytes 7113373 | solution.py:135
  85.6 0.1 copy.55
  85.8 0.5 convolution_add_fusion.3
  86.3 0.4 multiply_reduce_fusion.3
  86.7 0.7 select_reduce_fusion.2
  87.4 0.4 fusion.68
  87.9 0.3 fusion.69
  88.3 0.1 copy.58
  88.5 0.1 copy.57
  88.7 0.6 fusion.70
  89.4 0.1 copy.55
  89.6 0.5 convolution_add_fusion.3
  90.1 0.4 multiply_reduce_fusion.3
  90.5 0.7 select_reduce_fusion.2
  91.2 0.4 fusion.68
  91.7 0.3 fusion.69
  92.1 0.1 copy.58
  92.3 0.1 copy.57
  92.5 0.6 fusion.70
  93.1 0.7 copy-done.1
  93.8 0.3 fusion.38
  94.1 9.6 %all-gather = f32[1024,8]{0,1:T(8,128)S(1)} all-gather(f32[256,8]{0,1:T(8,128)S(1)} %get-tuple-element.242), channel_id=2, replica_groups=mesh['node'=128,'hub'=4] {'hub'}, dimensions={0}, use_global_device_ids=true | all-gather | bytes 40960 | tf_op jit(solution)/shard_map/all_gather | solution.py:10
  103.7 9.8 %all-gather.1 = f32[1024,8]{0,1:T(8,128)S(1)} all-gather(f32[256,8]{0,1:T(8,128)S(1)} %get-tuple-element.243), channel_id=3, replica_groups=mesh['node'=128,'hub'=4] {'hub'}, dimensions={0}, use_global_device_ids=true | all-gather | bytes 40960 | tf_op jit(solution)/shard_map/all_gather | solution.py:10
  113.5 4.2 %all-gather.5.cloned.1.call-done = f32[1024,256]{1,0:T(8,128)} async-done(((f32[256,256]{1,0:T(8,128)}), f32[1024,256]{1,0:T(8,128)}) %all-gather.5.cloned.1.call-update) | async-done | bytes 1048592 | tf_op jit(solution)/shard_map/all_gather | solution.py:10
  117.6 1.0 slice.47
  118.6 0.1 copy.45
  118.8 3.8 %while.34 = (s32[]{:T(128)}, f32[256,8]{0,1:T(8,128)S(1)}, f32[256,8]{0,1:T(8,128)S(1)}, f32[256,256]{0,1:T(8,128)S(1)}, f32[4,256,8]{1,2,0:T(8,128)S(1)}, /*ind...) while((s32[]{:T(128)}, f32[256,8]{0,1:T(8,128)S(1)}, ...), condition=%wide.region_5.6_spmd, body=%wide.region_4.5_spmd.sunk | while | flops 208901 | bytes 1917071 | solution.py:16
  118.8 1.0 constant_dynamic-slice_fusion.7
  119.8 0.1 copy.54
  120.0 0.1 fusion.62
  120.1 1.0 constant_dynamic-slice_fusion.7
  121.1 0.1 copy.54
  121.2 0.1 fusion.62
  121.4 1.0 constant_dynamic-slice_fusion.7
  122.4 0.1 copy.54
  122.5 0.1 fusion.62
  122.7 0.3 fusion.37
  123.0 0.8 fusion.23
  (62 shorter events, 1.2 us)
Async XLA Ops:
  6.5 87.3 %copy-start = (bf16[256,768]{1,0:T(8,128)(2,1)S(1)}, bf16[256,768]{1,0:T(8,128)(2,1)}, u32[]{:S(2)}) copy-start(bf16[256,768]{1,0:T(8,128)(2,1)} %param.21) | copy-start | bytes 1179652
  8.1 35.2 %all-to-all-start = ((s32[128,1,8]{2,1,0:T(1,128)}), s32[128,1,8]{2,1,0:T(1,128)S(1)}, u32[]{:S(2)}, u32[]{:S(2)}) async-start(s32[128,1,8]{2,1,0:T(1,128)} %bitcast.5), calls=%async_computation | async-start | bytes 131072 | tf_op jit(solution)/shard_map/all_to_all | solution.py:113
  48.4 6.0 %copy-start.7 = (s32[1024]{0:T(1024)S(1)}, s32[1024]{0:T(1024)}, u32[]{:S(2)}) copy-start(s32[1024]{0:T(1024)} %param.23) | copy-start | bytes 12292
  48.4 6.0 %copy-start.8 = (s32[1024]{0:T(1024)S(1)}, s32[1024]{0:T(1024)}, u32[]{:S(2)}) copy-start(s32[1024]{0:T(1024)} %param.24) | copy-start | bytes 12292
  48.4 6.0 %copy-start.9 = (s32[1024]{0:T(1024)S(1)}, s32[1024]{0:T(1024)}, u32[]{:S(2)}) copy-start(s32[1024]{0:T(1024)} %param.25) | copy-start | bytes 12292
  48.4 6.1 %copy-start.6 = (bf16[4,256]{1,0:T(4,128)(2,1)S(1)}, bf16[4,256]{1,0:T(4,128)(2,1)}, u32[]{:S(2)}) copy-start(bf16[4,256]{1,0:T(4,128)(2,1)} %param.18) | copy-start | bytes 6148
  48.4 6.1 %copy-start.2 = (bf16[256,256]{1,0:T(8,128)(2,1)S(1)}, bf16[256,256]{1,0:T(8,128)(2,1)}, u32[]{:S(2)}) copy-start(bf16[256,256]{1,0:T(8,128)(2,1)} %param.15) | copy-start | bytes 393220
  48.4 6.1 %copy-start.4 = (f32[8,32]{1,0:T(8,128)S(1)}, f32[8,32]{1,0:T(8,128)}, u32[]{:S(2)}) copy-start(f32[8,32]{1,0:T(8,128)} %param.19) | copy-start | bytes 3076
  48.4 6.1 %copy-start.5 = (bf16[256,256]{1,0:T(8,128)(2,1)S(1)}, bf16[256,256]{1,0:T(8,128)(2,1)}, u32[]{:S(2)}) copy-start(bf16[256,256]{1,0:T(8,128)(2,1)} %param.17) | copy-start | bytes 393220
  48.4 37.0 %all-to-all-start.1 = ((bf16[128,8,256]{2,1,0:T(8,128)(2,1)}), bf16[128,8,256]{2,1,0:T(8,128)(2,1)S(1)}, u32[]{:S(2)}, u32[]{:S(2)}) async-start(bf16[128,8,256]{2,1,0:T(8,128)(2,1)} %bitcast.7), calls=%async_computation.1 | async-start | bytes 1048576 | tf_op jit(solution)/shard_map/all_to_all | solution.py:112
  54.3 63.3 %all-gather.5.cloned.1.call-start = ((), (), s32[]{:S(2)}) async-start(), calls=%async_computation.2 | async-start | bytes 1310720 | tf_op jit(solution)/shard_map/all_gather | solution.py:10
  93.1 0.7 copy-start.1
  118.8 3.9 %copy-start.3 = (bf16[256,768]{1,0:T(8,128)(2,1)S(1)}, bf16[256,768]{1,0:T(8,128)(2,1)}, u32[]{:S(2)}) copy-start(bf16[256,768]{1,0:T(8,128)(2,1)} %param.20) | copy-start | bytes 1179652
Sparse Core Ops, SparseCore 0:
  93.9 23.6 all-gather.4
where the time goes:
time: 133 us; the launch traced here: 131 us
  waiting for transfers between devices  48.3 us (36%)
  starting transfers between devices  26.3 us (20%)
  blocking collectives  19.3 us (15%)
  between operations  13.7 us (10%)
  local copies, waits for them, and re-layouts  12.6 us (9%)
  matrix products  6.47 us (5%)
  other arithmetic  3.68 us (3%)
    all_to_all x1, waiting for transfers between devices, body(): lax.all_to_all(source[lax.all_to_all(local_src, 'node', split_axis=0, con...  30.6 us
    all_to_all x1, starting transfers between devices, body(): lax.all_to_all(local_src, 'node', split_axis=0, concat_axis=0, tiled=True)  20.4 us
    all_gather x2, blocking collectives, merged_2(): everything = jax.tree.map(lambda part: lax.all_gather(part, axis), shard)  19.3 us
    all_to_all x1, waiting for transfers between devices, body(): lax.all_to_all(local_src, 'node', split_axis=0, concat_axis=0, tiled=True)  13.5 us
    all_to_all x1, starting transfers between devices, body(): lax.all_to_all(source[lax.all_to_all(local_src, 'node', split_axis=0, con...  5.85 us
    gather x1, local copies, waits for them, and re-layouts, body(): source[lax.all_to_all(local_src, 'node', split_axis=0, concat_axis=0, til...  4.97 us
    all_gather x1, waiting for transfers between devices, merged_2(): everything = jax.tree.map(lambda part: lax.all_gather(part, axis), shard)  4.19 us
    dynamic_slice x6, local copies, waits for them, and re-layouts, hop(): return combine(so_far, jax.tree.map(lambda part: part[k], everything))  3.35 us
  transfers between devices with their start and end apart: 3, of which 3 were waited for; matrix products, arithmetic and copies ran while one was open for 2% of the time, Pallas kernels for 0%

commit v1 on v0

v1 whole, which is shorter than its diff:
```python
import functools

import jax
import jax.numpy as jnp
from jax import lax
from jax.experimental import pallas as pl
from jax.experimental.pallas import tpu as pltpu
from jax.sharding import PartitionSpec as P

f32 = jnp.float32
bf16 = jnp.bfloat16
big_value = 1e30
MESH = pl.DeviceIdType.MESH
GROUP = 128


def halves(x):
    high = x.astype(bf16)
    return high, (x - high.astype(f32)).astype(bf16)


def dot(a, b):
    return jnp.dot(a, b, preferred_element_type=f32)


def dot_nt(a, b):
    return lax.dot_general(a, b, (((1,), (1,)), ((), ())), preferred_element_type=f32)


def leaky(v):
    return jnp.maximum(v, 0.2 * v)


def lane_ids(rows, lanes):
    return lax.broadcasted_iota(jnp.int32, (rows, lanes), 1).astype(f32)


def columns(flat):
    return jnp.transpose(flat.astype(f32))


def requests(src_cols, slots, node_dev):
    lanes, groups = src_cols.shape
    per = lanes // slots
    cube = src_cols.reshape(per, slots, groups)
    low = jnp.min(cube, axis=1)
    high = jnp.max(cube, axis=1)
    picked = jnp.where(cube == jnp.max(cube, axis=1, keepdims=True), 1.0, 0.0).reshape(lanes, groups)
    lane = lax.broadcasted_iota(jnp.int32, (per, 128), 1)
    row = lax.broadcasted_iota(jnp.int32, (per, 128), 0)
    out = []
    for g in range(groups):
        first = ((g * per + row) * node_dev).astype(f32)
        out.append(jnp.where(lane == 0, low[:, g : g + 1], high[:, g : g + 1]) - first)
    return out, picked


def owner_rows(asked, source):
    peers, node_dev = asked.shape[0], source.shape[0]
    ids = lane_ids(peers, node_dev)
    first = dot(jnp.where(ids == asked[:, 0:1], 1.0, 0.0).astype(bf16), source)
    second = dot(jnp.where(ids == asked[:, 1:2], 1.0, 0.0).astype(bf16), source)
    return jnp.stack([first, second], axis=1).astype(bf16)


def head_matrix(attention, width):
    heads, head_dim = attention.shape
    wide = jnp.concatenate([attention] * heads, axis=1)
    return jnp.where(head_mask(heads, width), wide, 0.0)


def head_mask(heads, width):
    head_dim = width // heads
    lane = lax.broadcasted_iota(jnp.int32, (heads, width), 1)
    row = lax.broadcasted_iota(jnp.int32, (heads, width), 0)
    return (lane >= row * head_dim) & (lane < (row + 1) * head_dim)


def scores(left, att_high, att_low):
    high, low = halves(left)
    return dot_nt(high, att_high) + (dot_nt(high, att_low) + dot_nt(low, att_high))


def scores_t(left, att_high, att_low):
    high, low = halves(left)
    return dot_nt(att_high, high) + (dot_nt(att_low, high) + dot_nt(att_high, low))


def merge(peaks, totals, values, self_t, source, expand):
    peak = self_t
    for p in peaks:
        peak = jnp.maximum(peak, p)
    scales = [jnp.exp(p - peak) for p in peaks]
    self_scale = jnp.exp(self_t - peak)
    total = self_scale
    for s, t in zip(scales, totals):
        total = total + s * t
    inverse = 1.0 / total
    coefs = jnp.concatenate([s * inverse for s in scales] + [self_scale * inverse], axis=0)
    high, low = halves(jnp.transpose(coefs))
    heads = self_t.shape[0]
    agg = None
    for d, value in enumerate(list(values) + [source]):
        part = slice(d * heads, (d + 1) * heads)
        factor = dot(high[:, part], expand) + dot(low[:, part], expand)
        term = factor * value.astype(f32)
        agg = term if agg is None else agg + term
    return agg.astype(bf16)


def gru(agg, from_state, state, w_input):
    width = state.shape[1]
    from_input = dot(agg, w_input)
    reset = jax.nn.sigmoid(from_input[:, :width] + from_state[:, :width])
    update = jax.nn.sigmoid(from_input[:, width : 2 * width] + from_state[:, width : 2 * width])
    candidate = jnp.tanh(from_input[:, 2 * width :] + reset * from_state[:, 2 * width :])
    return ((1.0 - update) * candidate + update * state.astype(f32)).astype(bf16)


def kernel(
    peers,
    hubs,
    state_ref,
    w_source_ref,
    w_target_ref,
    type_ref,
    attention_ref,
    w_input_ref,
    w_hidden_ref,
    src_ref,
    dst_ref,
    kind_ref,
    live_ref,
    out_ref,
    ask_out,
    ask_in,
    row_out,
    row_in,
    source_ref,
    member_ref,
    member_t_ref,
    pick_ref,
    base_ref,
    mask_ref,
    dead_ref,
    score_ref,
    rows_ref,
    value_ref,
    stat_ref,
    value_in,
    stat_in,
    from_state_ref,
    ask_send,
    ask_recv,
    ask_own,
    row_send,
    row_recv,
    row_own,
    value_send,
    value_recv,
    stat_send,
    stat_recv,
):
    me = lax.axis_index("node")
    hub = lax.axis_index("hub")
    node_dev, width = state_ref.shape
    heads = attention_ref.shape[0]
    groups = src_ref.shape[0]
    slots = groups * 128 // peers

    def each_peer(act):
        act(lax.rem(me + peers // 2, peers))

        def step(t, carry):
            act(lax.rem(me + (peers // 2 + 1 + t), peers))
            act(lax.rem(me + (peers // 2 - 1 - t), peers))
            return carry

        lax.fori_loop(0, peers // 2 - 1, step, 0)

    barrier = pltpu.get_barrier_semaphore()

    def greet(peer):
        pl.semaphore_signal(barrier, inc=1, device_id=(peer, hub), device_id_type=MESH)

    each_peer(greet)
    for h in range(1, hubs):
        pl.semaphore_signal(
            barrier, inc=1, device_id=(me, lax.rem(hub + h, hubs)), device_id_type=MESH
        )

    asks, picked = requests(columns(src_ref[...]), slots, node_dev)
    per = peers // groups
    for g in range(groups):
        ask_out[g * per : (g + 1) * per, 0, :] = asks[g]
    state = state_ref[...]
    source = dot(state, w_source_ref[...]).astype(bf16)
    source_ref[...] = source

    pl.semaphore_wait(barrier, peers - 1 + hubs - 1)

    def ask(peer):
        pltpu.make_async_remote_copy(
            src_ref=ask_out.at[peer],
            dst_ref=ask_in.at[me],
            send_sem=ask_send,
            recv_sem=ask_recv,
            device_id=(peer, hub),
            device_id_type=MESH,
        ).start()

    each_peer(ask)
    own_ask = pltpu.make_async_copy(ask_out.at[me], ask_in.at[me], ask_own)
    own_ask.start()

    target = dot(state, w_target_ref[...])
    target_high, target_low = halves(target)
    types = type_ref[...].astype(f32)
    att = head_matrix(attention_ref[...], width)
    att_high, att_low = halves(att)
    expand = jnp.where(head_mask(heads, width), 1.0, 0.0).astype(bf16)
    self_t = scores_t(
        leaky(source.astype(f32) + target + types[types.shape[0] - 1 :, :]), att_high, att_low
    )
    dst_cols = columns(dst_ref[...])
    kind_cols = columns(kind_ref[...])
    live_cols = columns(live_ref[...])
    ids = lane_ids(GROUP, node_dev)
    block = (lax.broadcasted_iota(jnp.int32, (GROUP, 1), 0) // slots).astype(f32)
    node_ids = lax.broadcasted_iota(jnp.int32, (node_dev, GROUP), 0)
    for g in range(groups):
        part = slice(g * GROUP, (g + 1) * GROUP)
        here = ids == dst_cols[:, g : g + 1]
        member = jnp.where(here, 1.0, 0.0).astype(bf16)
        member_ref[part, :] = member
        mask_ref[part, :] = jnp.where(here, 0.0, -big_value)
        member_t_ref[:, part] = jnp.where(node_ids == dst_ref[g : g + 1, :], 1.0, 0.0).astype(bf16)
        wanted = 2.0 * (g * (GROUP // slots) + block) + picked[:, g : g + 1]
        pick_ref[part, :] = jnp.where(lane_ids(GROUP, 2 * peers) == wanted, 1.0, 0.0).astype(bf16)
        kind = kind_cols[:, g : g + 1]
        kinds = types[0:1, :]
        for t in range(1, types.shape[0]):
            kinds = jnp.where(kind == float(t), types[t : t + 1, :], kinds)
        base_ref[part, :] = dot(member, target_high) + dot(member, target_low) + kinds
        dead_ref[part, :] = jnp.broadcast_to(
            jnp.where(live_cols[:, g : g + 1] > 0.0, 0.0, -big_value), (GROUP, heads)
        )

    own_ask.wait()
    pltpu.make_async_copy(
        ask_in.at[pl.ds(0, peers - 1)], ask_in.at[pl.ds(0, peers - 1)], ask_recv
    ).wait()
    row_out[...] = owner_rows(ask_in[:, 0, :], source_ref[...])

    def reply(peer):
        pltpu.make_async_remote_copy(
            src_ref=row_out.at[peer],
            dst_ref=row_in.at[me],
            send_sem=row_send,
            recv_sem=row_recv,
            device_id=(peer, hub),
            device_id_type=MESH,
        ).start()

    each_peer(reply)
    own_row = pltpu.make_async_copy(row_out.at[me], row_in.at[me], row_own)
    own_row.start()
    from_state_ref[...] = dot(state_ref[...], w_hidden_ref[...])
    pltpu.make_async_copy(
        ask_out.at[pl.ds(0, peers - 1)], ask_out.at[pl.ds(0, peers - 1)], ask_send
    ).wait()
    own_row.wait()
    pltpu.make_async_copy(
        row_in.at[pl.ds(0, peers - 1)], row_in.at[pl.ds(0, peers - 1)], row_recv
    ).wait()

    fetched = row_in[...].reshape(2 * peers, width)

    def score_step(g, peaks):
        part = pl.ds(pl.multiple_of(g * GROUP, GROUP), GROUP)
        rows = dot(pick_ref[part, :], fetched)
        rows_ref[part, :] = rows.astype(bf16)
        score = scores(leaky(rows + base_ref[part, :]), att_high, att_low) + dead_ref[part, :]
        score_ref[part, :] = score
        mask = mask_ref[part, :]
        fresh = [jnp.max(score[:, h : h + 1] + mask, axis=0, keepdims=True) for h in range(heads)]
        return jnp.maximum(peaks, jnp.concatenate(fresh, axis=0))

    peak = lax.fori_loop(0, groups, score_step, self_t)
    peak_high, peak_low = halves(peak)
    peak = peak_high.astype(f32) + peak_low.astype(f32)

    def weigh_step(g, carry):
        value, total = carry
        part = pl.ds(pl.multiple_of(g * GROUP, GROUP), GROUP)
        member = member_ref[part, :]
        edge_peak = dot_nt(member, peak_high) + dot_nt(member, peak_low)
        weight = jnp.exp(score_ref[part, :] - edge_peak).astype(bf16)
        weighted = (dot(weight, expand) * rows_ref[part, :].astype(f32)).astype(bf16)
        member_t = member_t_ref[:, part]
        return value + dot(member_t, weighted), total + dot(member_t, weight)

    value, total = lax.fori_loop(
        0,
        groups,
        weigh_step,
        (jnp.zeros((node_dev, width), f32), jnp.zeros((node_dev, heads), f32)),
    )
    value_ref[...] = value.astype(bf16)
    stat_ref[0:heads, :] = peak
    stat_ref[heads : 2 * heads, :] = jnp.transpose(total)

    copies = []
    for h in range(1, hubs):
        other = (me, lax.rem(hub + h, hubs))
        for source_buf, target_buf, send, recv in (
            (stat_ref, stat_in, stat_send, stat_recv),
            (value_ref, value_in, value_send, value_recv),
        ):
            copy = pltpu.make_async_remote_copy(
                src_ref=source_buf,
                dst_ref=target_buf.at[h - 1],
                send_sem=send.at[h - 1],
                recv_sem=recv.at[h - 1],
                device_id=other,
                device_id_type=MESH,
            )
            copy.start()
            copies.append(copy)
    for copy in copies:
        copy.wait()
    pltpu.make_async_copy(
        row_out.at[pl.ds(0, peers - 1)], row_out.at[pl.ds(0, peers - 1)], row_send
    ).wait()

    stats = [stat_ref[...]] + [stat_in[h] for h in range(hubs - 1)]
    agg = merge(
        [s[0:heads, :] for s in stats],
        [s[heads : 2 * heads, :] for s in stats],
        [value_ref[...]] + [value_in[h] for h in range(hubs - 1)],
        self_t,
        source_ref[...],
        expand,
    )
    out_ref[...] = gru(agg, from_state_ref[...], state_ref[...], w_input_ref[...])


def body(
    node_state,
    w_source,
    w_target,
    type_table,
    attention,
    w_input,
    w_hidden,
    edge_src,
    edge_dst,
    edge_type,
    edge_live,
):
    peers = lax.axis_size("node")
    hubs = lax.axis_size("hub")
    node_dev, width = node_state.shape
    heads = attention.shape[0]
    edges = edge_src.shape[0]
    dma = pltpu.SemaphoreType.DMA
    vmem = pltpu.VMEM
    return pl.pallas_call(
        functools.partial(kernel, peers, hubs),
        out_shape=jax.ShapeDtypeStruct((node_dev, width), bf16),
        in_specs=[pl.BlockSpec(memory_space=pltpu.VMEM)] * 11,
        out_specs=pl.BlockSpec(memory_space=pltpu.VMEM),
        scratch_shapes=[
            vmem((peers, 1, 128), f32),
            vmem((peers, 1, 128), f32),
            vmem((peers, 2, width), bf16),
            vmem((peers, 2, width), bf16),
            vmem((node_dev, width), bf16),
            vmem((edges, node_dev), bf16),
            vmem((node_dev, edges), bf16),
            vmem((edges, 2 * peers), bf16),
            vmem((edges, width), f32),
            vmem((edges, node_dev), f32),
            vmem((edges, heads), f32),
            vmem((edges, heads), f32),
            vmem((edges, width), bf16),
            vmem((node_dev, width), bf16),
            vmem((2 * heads, node_dev), f32),
            vmem((hubs - 1, node_dev, width), bf16),
            vmem((hubs - 1, 2 * heads, node_dev), f32),
            vmem((node_dev, 3 * width), f32),
            dma,
            dma,
            dma,
            dma,
            dma,
            dma,
            dma((hubs - 1,)),
            dma((hubs - 1,)),
            dma((hubs - 1,)),
            dma((hubs - 1,)),
        ],
        compiler_params=pltpu.CompilerParams(collective_id=0, has_side_effects=True),
        name="gat",
    )(
        node_state,
        w_source,
        w_target,
        type_table,
        attention,
        w_input,
        w_hidden,
        edge_src.reshape(-1, 128),
        edge_dst.reshape(-1, 128),
        edge_type.reshape(-1, 128),
        edge_live.reshape(-1, 128),
    )


def solution(mesh):
    edges = P(("node", "hub"))
    placed = (P("node", None), P(), P(), P(), P(), P(), P(), edges, edges, edges, edges)
    return jax.shard_map(
        body, mesh=mesh, in_specs=placed, out_specs=P("node", None), check_vma=False
    )
```

time: 133 us -> 59.9 us (0.45); the launches traced: 131 us -> 59.8 us
  Pallas kernels: 0 us -> 58.2 us
  waiting for transfers between devices: 48.3 us -> 0 us
  starting transfers between devices: 26.3 us -> 0 us
  blocking collectives: 19.3 us -> 0 us
  between operations: 13.7 us -> 0.01 us
  local copies, waits for them, and re-layouts: 12.6 us -> 1.57 us
  matrix products: 6.47 us -> 0 us
  other arithmetic: 3.68 us -> 0 us
    pallas_call x0 -> x1, Pallas kernels: none -> 58.2 us  [body(): pl.pallas_call(functools.partial(kernel, peers, hubs), out_shape=jax.Shap...]
    all_to_all x2 -> x0, waiting for transfers between devices: 44.1 us -> none  [the longest x1 30.6 us: body(): lax.all_to_all(source[lax.all_to_all(local_src, 'node', split_axis=0, con...]
    all_to_all x2 -> x0, starting transfers between devices: 26.2 us -> none  [the longest x1 20.4 us: body(): lax.all_to_all(local_src, 'node', split_axis=0, concat_axis=0, tiled=True)]
    all_gather x2 -> x0, blocking collectives: 19.3 us -> none  [merged_2(): everything = jax.tree.map(lambda part: lax.all_gather(part, axis), shard)]
    dot_general x14 -> x0, matrix products: 6.47 us -> none  [the longest x2 1.19 us: edge_partial(): jnp.dot(onehot.T, spread(weight, head_dim) * wide_rows, precision=highest...]
    gather x1 -> x0, local copies, waits for them, and re-layouts: 4.97 us -> none  [body(): source[lax.all_to_all(local_src, 'node', split_axis=0, concat_axis=0, til...]
    all_gather x1 -> x0, waiting for transfers between devices: 4.19 us -> none  [merged_2(): everything = jax.tree.map(lambda part: lax.all_gather(part, axis), shard)]
    dynamic_slice x12 -> x0, local copies, waits for them, and re-layouts: 3.7 us -> none  [the longest x6 3.35 us: hop(): return combine(so_far, jax.tree.map(lambda part: part[k], everything))]
  transfers between devices with their start and end apart: 3 -> 0, of which waited for: 3 -> 0; matrix products, arithmetic and copies ran while one was open for 2% -> 0% of each run, Pallas kernels for 0% -> 0%
where the time goes in v1:
time: 59.9 us; the launch traced here: 59.8 us
  Pallas kernels  58.2 us (97%)
  local copies, waits for them, and re-layouts  1.57 us (3%)
    pallas_call x1, Pallas kernels, body(): pl.pallas_call(functools.partial(kernel, peers, hubs), out_shape=jax.Shap...  58.2 us
    unnamed x1, local copies, waits for them, and re-layouts  1.57 us

profile of v1, /device:TPU:1, one launch (start us, length us, event | category | flops | bytes accessed | tf_op | source)
XLA Modules:
  0.0 59.8 jit_solution(9009451161149558602)
XLA Ops:
  0.0 58.2 %gat.1 = bf16[256,256]{1,0:T(8,128)(2,1)} custom-call(bf16[256,256]{1,0:T(8,128)(2,1)} %state_ref.1, bf16[256,256]{1,0:T(8,128)(2,1)} %w_source_ref.1, bf16[256,256]{1,0:T(8,128)(2,1)} %w_target_ref.1, bf16[4,256]{1,0:T(4,128)(2,1)} %type_ref.1, f32[8,32]{1,0:T(8,128)} %attention_ref.1, bf16[256,768]{1,0:T(8,128)(2,1)} %w_input_ref.1, ...), custom_call_target="tpu_custom_call" | custom-call | tf_op jit(solution)/shard_map/gat/pallas_call | solution.py:368
  58.2 1.6 %copy.13 = bf16[256,256]{1,0:T(8,128)(2,1)} copy(bf16[256,256]{1,0:T(8,128)(2,1)} %gat.1) | data formatting | bytes 262144

commit v2 on v1

--- a/solution.py
+++ b/solution.py
@@ -150,6 +150,8 @@
     value_in,
     stat_in,
     from_state_ref,
+    self_ref,
+    done_ref,
     ask_send,
     ask_recv,
     ask_own,
@@ -160,6 +162,8 @@
     value_recv,
     stat_send,
     stat_recv,
+    done_send,
+    done_recv,
 ):
     me = lax.axis_index("node")
     hub = lax.axis_index("hub")
@@ -307,42 +311,67 @@
         (jnp.zeros((node_dev, width), f32), jnp.zeros((node_dev, heads), f32)),
     )
     value_ref[...] = value.astype(bf16)
-    stat_ref[0:heads, :] = peak
-    stat_ref[heads : 2 * heads, :] = jnp.transpose(total)
+    quarter = node_dev // hubs
+    total_t = jnp.transpose(total)
+    for h in range(hubs):
+        nodes = slice(h * quarter, (h + 1) * quarter)
+        stat_ref[h, 0:heads, 0:quarter] = peak[:, nodes]
+        stat_ref[h, heads : 2 * heads, 0:quarter] = total_t[:, nodes]
+        self_ref[h, :, 0:quarter] = self_t[:, nodes]
 
     copies = []
     for h in range(1, hubs):
-        other = (me, lax.rem(hub + h, hubs))
+        other = lax.rem(hub + h, hubs)
+        theirs = pl.ds(pl.multiple_of(other * quarter, quarter), quarter)
         for source_buf, target_buf, send, recv in (
-            (stat_ref, stat_in, stat_send, stat_recv),
-            (value_ref, value_in, value_send, value_recv),
+            (stat_ref.at[other], stat_in, stat_send, stat_recv),
+            (value_ref.at[theirs, :], value_in, value_send, value_recv),
         ):
             copy = pltpu.make_async_remote_copy(
                 src_ref=source_buf,
                 dst_ref=target_buf.at[h - 1],
                 send_sem=send.at[h - 1],
                 recv_sem=recv.at[h - 1],
-                device_id=other,
+                device_id=(me, other),
                 device_id_type=MESH,
             )
             copy.start()
             copies.append(copy)
-    for copy in copies:
-        copy.wait()
     pltpu.make_async_copy(
         row_out.at[pl.ds(0, peers - 1)], row_out.at[pl.ds(0, peers - 1)], row_send
     ).wait()
-
-    stats = [stat_ref[...]] + [stat_in[h] for h in range(hubs - 1)]
+    mine = pl.ds(pl.multiple_of(hub * quarter, quarter), quarter)
+    own_stat = stat_ref[hub][:, 0:quarter]
+    own_self = self_ref[hub][:, 0:quarter]
+    own_value = value_ref[mine, :]
+    for copy in copies:
+        copy.wait()
+
+    stats = [own_stat] + [stat_in[h][:, 0:quarter] for h in range(hubs - 1)]
     agg = merge(
         [s[0:heads, :] for s in stats],
         [s[heads : 2 * heads, :] for s in stats],
-        [value_ref[...]] + [value_in[h] for h in range(hubs - 1)],
-        self_t,
-        source_ref[...],
+        [own_value] + [value_in[h] for h in range(hubs - 1)],
+        own_self,
+        source_ref[mine, :],
         expand,
     )
-    out_ref[...] = gru(agg, from_state_ref[...], state_ref[...], w_input_ref[...])
+    done_ref[...] = gru(agg, from_state_ref[mine, :], state_ref[mine, :], w_input_ref[...])
+    copies = []
+    for h in range(1, hubs):
+        copy = pltpu.make_async_remote_copy(
+            src_ref=done_ref,
+            dst_ref=out_ref.at[mine, :],
+            send_sem=done_send.at[h - 1],
+            recv_sem=done_recv.at[h - 1],
+            device_id=(me, lax.rem(hub + h, hubs)),
+            device_id_type=MESH,
+        )
+        copy.start()
+        copies.append(copy)
+    out_ref[mine, :] = done_ref[...]
+    for copy in copies:
+        copy.wait()
 
 
 def body(
@@ -363,6 +392,7 @@
     node_dev, width = node_state.shape
     heads = attention.shape[0]
     edges = edge_src.shape[0]
+    quarter = node_dev // hubs
     dma = pltpu.SemaphoreType.DMA
     vmem = pltpu.VMEM
     return pl.pallas_call(
@@ -385,16 +415,20 @@
             vmem((edges, heads), f32),
             vmem((edges, width), bf16),
             vmem((node_dev, width), bf16),
-            vmem((2 * heads, node_dev), f32),
-            vmem((hubs - 1, node_dev, width), bf16),
-            vmem((hubs - 1, 2 * heads, node_dev), f32),
+            vmem((hubs, 2 * heads, 128), f32),
+            vmem((hubs - 1, quarter, width), bf16),
+            vmem((hubs - 1, 2 * heads, 128), f32),
             vmem((node_dev, 3 * width), f32),
-            dma,
-            dma,
-            dma,
-            dma,
-            dma,
-            dma,
+            vmem((hubs, heads, 128), f32),
+            vmem((quarter, width), bf16),
+            dma,
+            dma,
+            dma,
+            dma,
+            dma,
+            dma,
+            dma((hubs - 1,)),
+            dma((hubs - 1,)),
             dma((hubs - 1,)),
             dma((hubs - 1,)),
             dma((hubs - 1,)),

time: 59.9 us -> 57.8 us (0.965)
  Pallas kernels: 58.2 us -> 56.1 us
    pallas_call x1, Pallas kernels: 58.2 us -> 56.1 us  [body(): pl.pallas_call(functools.partial(kernel, peers, hubs), out_shape=jax.Shap...]
where the time goes in v2:
time: 57.8 us; the launch traced here: 57.7 us
  Pallas kernels  56.1 us (97%)
  local copies, waits for them, and re-layouts  1.57 us (3%)
    pallas_call x1, Pallas kernels, body(): pl.pallas_call(functools.partial(kernel, peers, hubs), out_shape=jax.Shap...  56.1 us
    unnamed x1, local copies, waits for them, and re-layouts  1.57 us

profile of v2, /device:TPU:1, one launch (start us, length us, event | category | flops | bytes accessed | tf_op | source)
XLA Modules:
  0.0 57.7 jit_solution(16468659080014518961)
XLA Ops:
  0.0 56.1 %gat.1 = bf16[256,256]{1,0:T(8,128)(2,1)} custom-call(bf16[256,256]{1,0:T(8,128)(2,1)} %state_ref.1, bf16[256,256]{1,0:T(8,128)(2,1)} %w_source_ref.1, bf16[256,256]{1,0:T(8,128)(2,1)} %w_target_ref.1, bf16[4,256]{1,0:T(4,128)(2,1)} %type_ref.1, f32[8,32]{1,0:T(8,128)} %attention_ref.1, bf16[256,768]{1,0:T(8,128)(2,1)} %w_input_ref.1, ...), custom_call_target="tpu_custom_call" | custom-call | tf_op jit(solution)/shard_map/gat/pallas_call | solution.py:398
  56.1 1.6 %copy.13 = bf16[256,256]{1,0:T(8,128)(2,1)} copy(bf16[256,256]{1,0:T(8,128)(2,1)} %gat.1) | data formatting | bytes 262144

commit v3 on v2

--- a/solution.py
+++ b/solution.py
@@ -120,17 +120,17 @@
 def kernel(
     peers,
     hubs,
-    state_ref,
-    w_source_ref,
-    w_target_ref,
-    type_ref,
-    attention_ref,
-    w_input_ref,
-    w_hidden_ref,
-    src_ref,
-    dst_ref,
-    kind_ref,
-    live_ref,
+    state_any,
+    w_source_any,
+    w_target_any,
+    type_any,
+    attention_any,
+    w_input_any,
+    w_hidden_any,
+    src_any,
+    dst_any,
+    kind_any,
+    live_any,
     out_ref,
     ask_out,
     ask_in,
@@ -152,6 +152,8 @@
     from_state_ref,
     self_ref,
     done_ref,
+    weighted_ref,
+    weight_ref,
     ask_send,
     ask_recv,
     ask_own,
@@ -164,9 +166,38 @@
     stat_recv,
     done_send,
     done_recv,
+    load_sem,
+    state_ref,
+    w_source_ref,
+    w_target_ref,
+    type_ref,
+    attention_ref,
+    w_input_ref,
+    w_hidden_ref,
+    src_ref,
+    dst_ref,
+    kind_ref,
+    live_ref,
 ):
     me = lax.axis_index("node")
     hub = lax.axis_index("hub")
+    loads = {}
+    for i, (name, far, near) in enumerate(
+        (
+            ("state", state_any, state_ref),
+            ("w_source", w_source_any, w_source_ref),
+            ("w_target", w_target_any, w_target_ref),
+            ("type", type_any, type_ref),
+            ("attention", attention_any, attention_ref),
+            ("w_input", w_input_any, w_input_ref),
+            ("w_hidden", w_hidden_any, w_hidden_ref),
+            ("src", src_any, src_ref),
+            ("dst", dst_any, dst_ref),
+            ("kind", kind_any, kind_ref),
+            ("live", live_any, live_ref),
+        )
+    ):
+        loads[name] = pltpu.make_async_copy(far, near, load_sem.at[i])
     node_dev, width = state_ref.shape
     heads = attention_ref.shape[0]
     groups = src_ref.shape[0]
@@ -193,6 +224,13 @@
             barrier, inc=1, device_id=(me, lax.rem(hub + h, hubs)), device_id_type=MESH
         )
 
+    for name in ("src", "state", "w_source"):
+        loads[name].start()
+    for name in loads:
+        if name not in ("src", "state", "w_source"):
+            loads[name].start()
+    for name in ("src", "state", "w_source"):
+        loads[name].wait()
     asks, picked = requests(columns(src_ref[...]), slots, node_dev)
     per = peers // groups
     for g in range(groups):
@@ -217,6 +255,9 @@
     own_ask = pltpu.make_async_copy(ask_out.at[me], ask_in.at[me], ask_own)
     own_ask.start()
 
+    for name in loads:
+        if name not in ("src", "state", "w_source"):
+            loads[name].wait()
     target = dot(state, w_target_ref[...])
     target_high, target_low = halves(target)
     types = type_ref[...].astype(f32)
@@ -280,36 +321,29 @@
 
     fetched = row_in[...].reshape(2 * peers, width)
 
-    def score_step(g, peaks):
-        part = pl.ds(pl.multiple_of(g * GROUP, GROUP), GROUP)
+    peak = self_t
+    for g in range(groups):
+        part = slice(g * GROUP, (g + 1) * GROUP)
         rows = dot(pick_ref[part, :], fetched)
         rows_ref[part, :] = rows.astype(bf16)
         score = scores(leaky(rows + base_ref[part, :]), att_high, att_low) + dead_ref[part, :]
         score_ref[part, :] = score
         mask = mask_ref[part, :]
         fresh = [jnp.max(score[:, h : h + 1] + mask, axis=0, keepdims=True) for h in range(heads)]
-        return jnp.maximum(peaks, jnp.concatenate(fresh, axis=0))
-
-    peak = lax.fori_loop(0, groups, score_step, self_t)
+        peak = jnp.maximum(peak, jnp.concatenate(fresh, axis=0))
     peak_high, peak_low = halves(peak)
     peak = peak_high.astype(f32) + peak_low.astype(f32)
 
-    def weigh_step(g, carry):
-        value, total = carry
-        part = pl.ds(pl.multiple_of(g * GROUP, GROUP), GROUP)
+    for g in range(groups):
+        part = slice(g * GROUP, (g + 1) * GROUP)
         member = member_ref[part, :]
         edge_peak = dot_nt(member, peak_high) + dot_nt(member, peak_low)
         weight = jnp.exp(score_ref[part, :] - edge_peak).astype(bf16)
-        weighted = (dot(weight, expand) * rows_ref[part, :].astype(f32)).astype(bf16)
-        member_t = member_t_ref[:, part]
-        return value + dot(member_t, weighted), total + dot(member_t, weight)
-
-    value, total = lax.fori_loop(
-        0,
-        groups,
-        weigh_step,
-        (jnp.zeros((node_dev, width), f32), jnp.zeros((node_dev, heads), f32)),
-    )
+        weight_ref[part, :] = weight
+        rows = rows_ref[part, :].astype(f32)
+        weighted_ref[part, :] = (dot(weight, expand) * rows).astype(bf16)
+    total = dot(member_t_ref[...], weight_ref[...])
+    value = dot(member_t_ref[...], weighted_ref[...])
     value_ref[...] = value.astype(bf16)
     quarter = node_dev // hubs
     total_t = jnp.transpose(total)
@@ -393,12 +427,25 @@
     heads = attention.shape[0]
     edges = edge_src.shape[0]
     quarter = node_dev // hubs
+    inputs = (
+        node_state,
+        w_source,
+        w_target,
+        type_table,
+        attention,
+        w_input,
+        w_hidden,
+        edge_src.reshape(-1, 128),
+        edge_dst.reshape(-1, 128),
+        edge_type.reshape(-1, 128),
+        edge_live.reshape(-1, 128),
+    )
     dma = pltpu.SemaphoreType.DMA
     vmem = pltpu.VMEM
     return pl.pallas_call(
         functools.partial(kernel, peers, hubs),
         out_shape=jax.ShapeDtypeStruct((node_dev, width), bf16),
-        in_specs=[pl.BlockSpec(memory_space=pltpu.VMEM)] * 11,
+        in_specs=[pl.BlockSpec(memory_space=pl.ANY)] * 11,
         out_specs=pl.BlockSpec(memory_space=pltpu.VMEM),
         scratch_shapes=[
             vmem((peers, 1, 128), f32),
@@ -421,34 +468,26 @@
             vmem((node_dev, 3 * width), f32),
             vmem((hubs, heads, 128), f32),
             vmem((quarter, width), bf16),
-            dma,
-            dma,
-            dma,
-            dma,
-            dma,
-            dma,
-            dma((hubs - 1,)),
-            dma((hubs - 1,)),
-            dma((hubs - 1,)),
-            dma((hubs - 1,)),
-            dma((hubs - 1,)),
-            dma((hubs - 1,)),
+            vmem((edges, width), bf16),
+            vmem((edges, heads), bf16),
+            dma,
+            dma,
+            dma,
+            dma,
+            dma,
+            dma,
+            dma((hubs - 1,)),
+            dma((hubs - 1,)),
+            dma((hubs - 1,)),
+            dma((hubs - 1,)),
+            dma((hubs - 1,)),
+            dma((hubs - 1,)),
+            dma((len(inputs),)),
+            *[vmem(x.shape, x.dtype) for x in inputs],
         ],
         compiler_params=pltpu.CompilerParams(collective_id=0, has_side_effects=True),
         name="gat",
-    )(
-        node_state,
-        w_source,
-        w_target,
-        type_table,
-        attention,
-        w_input,
-        w_hidden,
-        edge_src.reshape(-1, 128),
-        edge_dst.reshape(-1, 128),
-        edge_type.reshape(-1, 128),
-        edge_live.reshape(-1, 128),
-    )
+    )(*inputs)
 
 
 def solution(mesh):

time: 57.8 us -> 52.4 us (0.907)
  Pallas kernels: 56.1 us -> 50.7 us
    pallas_call x1, Pallas kernels: 56.1 us -> 50.7 us  [body(): pl.pallas_call(functools.partial(kernel, peers, hubs), out_shape=jax.Shap...]
where the time goes in v3:
time: 52.4 us; the launch traced here: 52.2 us
  Pallas kernels  50.7 us (97%)
  local copies, waits for them, and re-layouts  1.57 us (3%)
    pallas_call x1, Pallas kernels, body(): pl.pallas_call(functools.partial(kernel, peers, hubs), out_shape=jax.Shap...  50.7 us
    unnamed x1, local copies, waits for them, and re-layouts  1.57 us

profile of v3, /device:TPU:1, one launch (start us, length us, event | category | flops | bytes accessed | tf_op | source)
XLA Modules:
  0.0 52.2 jit_solution(12665202349533179136)
XLA Ops:
  0.0 50.7 %gat.1 = bf16[256,256]{1,0:T(8,128)(2,1)} custom-call(bf16[256,256]{1,0:T(8,128)(2,1)} %state_any.1, bf16[256,256]{1,0:T(8,128)(2,1)} %w_source_any.1, bf16[256,256]{1,0:T(8,128)(2,1)} %w_target_any.1, bf16[4,256]{1,0:T(4,128)(2,1)} %type_any.1, f32[8,32]{1,0:T(8,128)} %attention_any.1, bf16[256,768]{1,0:T(8,128)(2,1)} %w_input_any.1, ...), custom_call_target="tpu_custom_call" | custom-call | tf_op jit(solution)/shard_map/gat/pallas_call | solution.py:445
  50.7 1.6 %copy.13 = bf16[256,256]{1,0:T(8,128)(2,1)} copy(bf16[256,256]{1,0:T(8,128)(2,1)} %gat.1) | data formatting | bytes 262144

commit v4 on v3

--- a/solution.py
+++ b/solution.py
@@ -349,12 +349,12 @@
     total_t = jnp.transpose(total)
     for h in range(hubs):
         nodes = slice(h * quarter, (h + 1) * quarter)
-        stat_ref[h, 0:heads, 0:quarter] = peak[:, nodes]
-        stat_ref[h, heads : 2 * heads, 0:quarter] = total_t[:, nodes]
+        stat_ref[h] = jnp.concatenate([peak[:, nodes], total_t[:, nodes]], axis=1)
         self_ref[h, :, 0:quarter] = self_t[:, nodes]
 
+    order = sorted(range(1, hubs), key=lambda h: abs(h - hubs / 2))
     copies = []
-    for h in range(1, hubs):
+    for h in order:
         other = lax.rem(hub + h, hubs)
         theirs = pl.ds(pl.multiple_of(other * quarter, quarter), quarter)
         for source_buf, target_buf, send, recv in (
@@ -375,16 +375,16 @@
         row_out.at[pl.ds(0, peers - 1)], row_out.at[pl.ds(0, peers - 1)], row_send
     ).wait()
     mine = pl.ds(pl.multiple_of(hub * quarter, quarter), quarter)
-    own_stat = stat_ref[hub][:, 0:quarter]
+    own_stat = stat_ref[hub]
     own_self = self_ref[hub][:, 0:quarter]
     own_value = value_ref[mine, :]
     for copy in copies:
         copy.wait()
 
-    stats = [own_stat] + [stat_in[h][:, 0:quarter] for h in range(hubs - 1)]
+    stats = [own_stat] + [stat_in[h] for h in range(hubs - 1)]
     agg = merge(
-        [s[0:heads, :] for s in stats],
-        [s[heads : 2 * heads, :] for s in stats],
+        [s[:, 0:quarter] for s in stats],
+        [s[:, quarter:] for s in stats],
         [own_value] + [value_in[h] for h in range(hubs - 1)],
         own_self,
         source_ref[mine, :],
@@ -392,7 +392,7 @@
     )
     done_ref[...] = gru(agg, from_state_ref[mine, :], state_ref[mine, :], w_input_ref[...])
     copies = []
-    for h in range(1, hubs):
+    for h in order:
         copy = pltpu.make_async_remote_copy(
             src_ref=done_ref,
             dst_ref=out_ref.at[mine, :],
@@ -462,9 +462,9 @@
             vmem((edges, heads), f32),
             vmem((edges, width), bf16),
             vmem((node_dev, width), bf16),
-            vmem((hubs, 2 * heads, 128), f32),
+            vmem((hubs, heads, 2 * quarter), f32),
             vmem((hubs - 1, quarter, width), bf16),
-            vmem((hubs - 1, 2 * heads, 128), f32),
+            vmem((hubs - 1, heads, 2 * quarter), f32),
             vmem((node_dev, 3 * width), f32),
             vmem((hubs, heads, 128), f32),
             vmem((quarter, width), bf16),

time: 52.4 us -> 51.9 us (level)
  Pallas kernels: 50.7 us -> 50.1 us
    pallas_call x1, Pallas kernels: 50.7 us -> 50.1 us  [body(): pl.pallas_call(functools.partial(kernel, peers, hubs), out_shape=jax.Shap...]
where the time goes in v4:
time: 51.9 us; the launch traced here: 51.6 us
  Pallas kernels  50.1 us (97%)
  local copies, waits for them, and re-layouts  1.57 us (3%)
    pallas_call x1, Pallas kernels, body(): pl.pallas_call(functools.partial(kernel, peers, hubs), out_shape=jax.Shap...  50.1 us
    unnamed x1, local copies, waits for them, and re-layouts  1.57 us

profile of v4, /device:TPU:1, one launch (start us, length us, event | category | flops | bytes accessed | tf_op | source)
XLA Modules:
  0.0 51.6 jit_solution(17597705742648272823)
XLA Ops:
  0.0 50.1 %gat.1 = bf16[256,256]{1,0:T(8,128)(2,1)} custom-call(bf16[256,256]{1,0:T(8,128)(2,1)} %state_any.1, bf16[256,256]{1,0:T(8,128)(2,1)} %w_source_any.1, bf16[256,256]{1,0:T(8,128)(2,1)} %w_target_any.1, bf16[4,256]{1,0:T(4,128)(2,1)} %type_any.1, f32[8,32]{1,0:T(8,128)} %attention_any.1, bf16[256,768]{1,0:T(8,128)(2,1)} %w_input_any.1, ...), custom_call_target="tpu_custom_call" | custom-call | tf_op jit(solution)/shard_map/gat/pallas_call | solution.py:445
  50.1 1.6 %copy.13 = bf16[256,256]{1,0:T(8,128)(2,1)} copy(bf16[256,256]{1,0:T(8,128)(2,1)} %gat.1) | data formatting | bytes 262144

commit v5 on v4

--- a/solution.py
+++ b/solution.py
@@ -343,8 +343,6 @@
         rows = rows_ref[part, :].astype(f32)
         weighted_ref[part, :] = (dot(weight, expand) * rows).astype(bf16)
     total = dot(member_t_ref[...], weight_ref[...])
-    value = dot(member_t_ref[...], weighted_ref[...])
-    value_ref[...] = value.astype(bf16)
     quarter = node_dev // hubs
     total_t = jnp.transpose(total)
     for h in range(hubs):
@@ -354,23 +352,31 @@
 
     order = sorted(range(1, hubs), key=lambda h: abs(h - hubs / 2))
     copies = []
+
+    def to_hub(h, source_buf, target_buf, send, recv):
+        copy = pltpu.make_async_remote_copy(
+            src_ref=source_buf,
+            dst_ref=target_buf,
+            send_sem=send,
+            recv_sem=recv,
+            device_id=(me, lax.rem(hub + h, hubs)),
+            device_id_type=MESH,
+        )
+        copy.start()
+        copies.append(copy)
+
     for h in order:
-        other = lax.rem(hub + h, hubs)
-        theirs = pl.ds(pl.multiple_of(other * quarter, quarter), quarter)
-        for source_buf, target_buf, send, recv in (
-            (stat_ref.at[other], stat_in, stat_send, stat_recv),
-            (value_ref.at[theirs, :], value_in, value_send, value_recv),
-        ):
-            copy = pltpu.make_async_remote_copy(
-                src_ref=source_buf,
-                dst_ref=target_buf.at[h - 1],
-                send_sem=send.at[h - 1],
-                recv_sem=recv.at[h - 1],
-                device_id=(me, other),
-                device_id_type=MESH,
-            )
-            copy.start()
-            copies.append(copy)
+        i = h - 1
+        theirs = stat_ref.at[lax.rem(hub + h, hubs)]
+        to_hub(h, theirs, stat_in.at[i], stat_send.at[i], stat_recv.at[i])
+    for c in range(2):
+        cols = slice(c * width // 2, (c + 1) * width // 2)
+        value_ref[:, cols] = dot(member_t_ref[...], weighted_ref[:, cols]).astype(bf16)
+        for h in order:
+            i = h - 1
+            start = lax.rem(hub + h, hubs) * quarter
+            theirs = value_ref.at[pl.ds(pl.multiple_of(start, quarter), quarter), cols]
+            to_hub(h, theirs, value_in.at[i, :, cols], value_send.at[c, i], value_recv.at[c, i])
     pltpu.make_async_copy(
         row_out.at[pl.ds(0, peers - 1)], row_out.at[pl.ds(0, peers - 1)], row_send
     ).wait()
@@ -476,8 +482,8 @@
             dma,
             dma,
             dma,
-            dma((hubs - 1,)),
-            dma((hubs - 1,)),
+            dma((2, hubs - 1)),
+            dma((2, hubs - 1)),
             dma((hubs - 1,)),
             dma((hubs - 1,)),
             dma((hubs - 1,)),

time: 51.9 us -> 51.9 us (level)
  no operation moved by 1% of the time
where the time goes in v5:
time: 51.9 us; the launch traced here: 51.8 us
  Pallas kernels  50.2 us (97%)
  local copies, waits for them, and re-layouts  1.57 us (3%)
    pallas_call x1, Pallas kernels, body(): pl.pallas_call(functools.partial(kernel, peers, hubs), out_shape=jax.Shap...  50.2 us
    unnamed x1, local copies, waits for them, and re-layouts  1.57 us

profile of v5, /device:TPU:1, one launch (start us, length us, event | category | flops | bytes accessed | tf_op | source)
XLA Modules:
  0.0 51.8 jit_solution(1584314320430797868)
XLA Ops:
  0.0 50.2 %gat.1 = bf16[256,256]{1,0:T(8,128)(2,1)} custom-call(bf16[256,256]{1,0:T(8,128)(2,1)} %state_any.1, bf16[256,256]{1,0:T(8,128)(2,1)} %w_source_any.1, bf16[256,256]{1,0:T(8,128)(2,1)} %w_target_any.1, bf16[4,256]{1,0:T(4,128)(2,1)} %type_any.1, f32[8,32]{1,0:T(8,128)} %attention_any.1, bf16[256,768]{1,0:T(8,128)(2,1)} %w_input_any.1, ...), custom_call_target="tpu_custom_call" | custom-call | tf_op jit(solution)/shard_map/gat/pallas_call | solution.py:451
  50.2 1.6 %copy.13 = bf16[256,256]{1,0:T(8,128)(2,1)} copy(bf16[256,256]{1,0:T(8,128)(2,1)} %gat.1) | data formatting | bytes 262144
